TPU v7x, 1024 devices: a whole 4x4x32 slice. The times are simulated.
1024 devices in a mesh: rows: 64 (over y, x, z_hi, core), depth: 16 (over z_lo).
Axes of the slice: x: 4, y: 4, z: 32 (z_hi: 2, z_lo: 16; z = z_hi * 16 + z_lo), core: 2. Of those that a mesh axis runs over, the one named last changes fastest.
Arguments:
- field: float32 [512, 256, 1024], P('rows', 'depth'), may hold values from 0 to 1
- diffusivity: bfloat16 [512, 256, 1024], P('rows', 'depth'), may hold values from 0.019897461 to 0.119628906
- velocity: bfloat16 [3, 512, 256, 1024], P(None, 'rows', 'depth'), may hold values from -1 to 1
Outputs:
- front: float32 [512, 256, 1024], P('rows', 'depth')
- picture: float32 [4, 512, 1024], P(None, 'rows', 'depth')
All inputs are finite; a program needn't handle non-finite values.
Results may differ from a plain program's by a relative error of at most 0.0003.
Values sent between devices are 32-bit elements; how exact they have to be, the bound alone decides.
A program may use at most 32 MiB of HBM per device.

v0:
```python
import jax
import jax.numpy as jnp
from jax import lax
from jax.sharding import PartitionSpec as P

time_step = 0.2
growth_rate = 1.0
opacity_total = 3.0


def extended_2(block, sides, width):
    for axis, dim in sides:
        count = lax.axis_size(axis)
        forward = [(i, i + 1) for i in range(count - 1)]
        backward = [(target, source) for source, target in forward]
        low = lax.ppermute(
            lax.slice_in_dim(block, block.shape[dim] - width, None, axis=dim), axis, forward
        )
        high = lax.ppermute(lax.slice_in_dim(block, 0, width, axis=dim), axis, backward)
        block = jnp.concatenate([low, block, high], axis=dim)
    return block


def swapped(value, axis, apart):
    return lax.ppermute(value, axis, [(i, i ^ 1 << apart) for i in range(lax.axis_size(axis))])


def upwind(speed, center, behind, ahead):
    return jnp.maximum(speed, 0.0) * (center - behind) + jnp.minimum(speed, 0.0) * (ahead - center)


def evolve(extended, diffusivity, velocity):
    padded = jnp.pad(extended, ((0, 0), (0, 0), (1, 1)))
    center = padded[1:-1, 1:-1, 1:-1]
    row_after = padded[2:, 1:-1, 1:-1]
    row_before = padded[:-2, 1:-1, 1:-1]
    deep_after = padded[1:-1, 2:, 1:-1]
    deep_before = padded[1:-1, :-2, 1:-1]
    col_after = padded[1:-1, 1:-1, 2:]
    col_before = padded[1:-1, 1:-1, :-2]
    laplace = (
        row_after + row_before + deep_after + deep_before + col_after + col_before - 6.0 * center
    )
    transport = upwind(velocity[0], center, row_before, row_after)
    transport = transport + upwind(velocity[1], center, deep_before, deep_after)
    transport = transport + upwind(velocity[2], center, col_before, col_after)
    return center + time_step * (
        diffusivity * laplace - transport + growth_rate * center * (1.0 - center)
    )


def render(extended, opacity):
    padded = jnp.pad(extended, ((0, 0), (0, 0), (1, 1)))
    center = padded[1:-1, 1:-1, 1:-1]
    grad_row = (padded[2:, 1:-1, 1:-1] - padded[:-2, 1:-1, 1:-1]) * 0.5
    grad_deep = (padded[1:-1, 2:, 1:-1] - padded[1:-1, :-2, 1:-1]) * 0.5
    grad_col = (padded[1:-1, 1:-1, 2:] - padded[1:-1, 1:-1, :-2]) * 0.5
    lighting = 0.48 * grad_row + 0.64 * grad_deep + 0.6 * grad_col
    magnitude = grad_row * grad_row + grad_deep * grad_deep + grad_col * grad_col + 0.1
    shade = 0.35 + 0.65 * lighting * lighting / magnitude
    optical = opacity * center
    through = jnp.cumsum(optical, axis=1)
    weight = jnp.exp(optical - through) * (1.0 - jnp.exp(-optical)) * shade
    red = jnp.sum(weight * center, axis=1)
    green = jnp.sum(weight * center * center, axis=1)
    blue = jnp.sum(weight * (1.0 - center), axis=1)
    remain = jnp.exp(-through[:, -1])
    return jnp.stack([red, green, blue, remain])


def over(nearer, farther):
    return jnp.concatenate(
        [nearer[:3] + nearer[3:] * farther[:3], nearer[3:] * farther[3:]], axis=0
    )


def shards(field, diffusivity, velocity):
    coef_diff = diffusivity.astype(jnp.float32)
    coef_vel = velocity.astype(jnp.float32)

    def advance(current):
        extended = extended_2(current, (("rows", 0), ("depth", 1)), 1)
        return evolve(extended, coef_diff, coef_vel)

    front = advance(advance(field))
    outlined = extended_2(front, (("rows", 0), ("depth", 1)), 1)
    groups = lax.axis_size("depth")
    depth_total = front.shape[1] * groups
    segment = render(outlined, opacity_total / depth_total)
    row_count = front.shape[0]
    col_width = front.shape[2] // groups
    levels = groups.bit_length() - 1
    position = lax.axis_index("depth")
    partial_value = segment.reshape((4, row_count) + (2,) * levels + (col_width,))
    for bit_index in range(levels):
        split_axis = 2 + (levels - 1 - bit_index)
        my_bit = position // 2**bit_index % 2
        keep_half = lax.dynamic_index_in_dim(partial_value, my_bit, split_axis, keepdims=False)
        give_half = lax.dynamic_index_in_dim(partial_value, 1 - my_bit, split_axis, keepdims=False)
        got_half = swapped(give_half, "depth", bit_index)
        nearer = jnp.where(my_bit == 0, keep_half, got_half)
        farther = jnp.where(my_bit == 0, got_half, keep_half)
        partial_value = over(nearer, farther)
    return (front, partial_value)


def solution(mesh):
    return jax.shard_map(
        shards,
        mesh=mesh,
        in_specs=(
            P("rows", "depth", None),
            P("rows", "depth", None),
            P(None, "rows", "depth", None),
        ),
        out_specs=(P("rows", "depth", None), P(None, "rows", "depth")),
        check_vma=False,
    )
```

profile of v0, /device:TPU:24, one launch (start us, length us, event | category | flops | bytes accessed | tf_op | source)
XLA Modules:
  0.0 206.5 jit_solution(495849807077327609)
XLA Ops:
  0.6 1.0 fusion.67
  1.7 30.8 %collective-permute-start = (f32[1,16,1024]{2,0,1:T(1,128)S(1)}, f32[1,16,1024]{2,0,1:T(1,128)S(1)}, u32[]{:S(2)}, u32[]{:S(2)}) collective-permute-start(f32[1,16,1024]{2,0,1:T(1,128)S(1)} %copy.24), channel_id=1, source_target_pairs={{16,0},{32,16},{48,32},{64,48},{80,64},{96,80},{112,96},{128,112},... | collective-permute-start | bytes 196616 | tf_op jit(solution)/shard_map/ppermute | solution.py:19
  32.5 0.1 copy.26
  32.5 1.9 collective-permute-start.1
  34.5 1.4 copy.39
  35.8 25.3 %collective-permute-done.1 = f32[1,16,1024]{2,0,1:T(1,128)S(1)} collective-permute-done((f32[1,16,1024]{2,0,1:T(1,128)S(1)}, f32[1,16,1024]{2,0,1:T(1,128)S(1)}, u32[]{:S(2)}, u32[]{:S(2)}) %collective-permute-start.1) | collective-permute-done | bytes 65568 | tf_op jit(solution)/shard_map/ppermute | solution.py:16
  61.2 1.3 collective-permute-start.2
  62.5 4.5 %collective-permute-start.3 = (f32[10,1,1024]{2,0,1:T(8,128)S(1)}, f32[10,1,1024]{2,0,1:T(8,128)S(1)}, u32[]{:S(2)}, u32[]{:S(2)}) collective-permute-start(f32[10,1,1024]{2,0,1:T(8,128)S(1)} %get-tuple-element.13), channel_id=1, source_target_pairs={{0,1},{1,2},{2,3},{3,4},{4,5},{5,6},{6,7},{7,8},{8,9},{9,10},{10,1... | collective-permute-start | bytes 122888 | tf_op jit(solution)/shard_map/ppermute | solution.py:16
  67.1 0.5 copy_convert_fusion
  67.6 1.4 collective-permute-done.3
  68.9 0.7 select_maximum_fusion.8
  69.7 1.0 fusion.4
  70.7 0.1 fusion.66
  70.8 5.0 %collective-permute-start.4 = (f32[1,16,1024]{2,0,1:T(1,128)S(1)}, f32[1,16,1024]{2,0,1:T(1,128)S(1)}, u32[]{:S(2)}, u32[]{:S(2)}) collective-permute-start(f32[1,16,1024]{2,0,1:T(1,128)S(1)} %get-tuple-element.17), channel_id=1, source_target_pairs={{16,0},{32,16},{48,32},{64,48},{80,64},{96,80},{112,96},{128,112},... | collective-permute-start | bytes 196616 | tf_op jit(solution)/shard_map/ppermute | solution.py:19
  75.8 1.9 collective-permute-start.5
  77.7 0.1 collective-permute-done.4
  77.9 25.0 %collective-permute-done.5 = f32[1,16,1024]{2,0,1:T(1,128)S(1)} collective-permute-done((f32[1,16,1024]{2,0,1:T(1,128)S(1)}, f32[1,16,1024]{2,0,1:T(1,128)S(1)}, u32[]{:S(2)}, u32[]{:S(2)}) %collective-permute-start.5) | collective-permute-done | bytes 65568 | tf_op jit(solution)/shard_map/ppermute | solution.py:16
  102.9 1.3 collective-permute-start.6
  104.2 4.5 %collective-permute-start.7 = (f32[10,1,1024]{2,0,1:T(8,128)S(1)}, f32[10,1,1024]{2,0,1:T(8,128)S(1)}, u32[]{:S(2)}, u32[]{:S(2)}) collective-permute-start(f32[10,1,1024]{2,0,1:T(8,128)S(1)} %get-tuple-element.11), channel_id=1, source_target_pairs={{0,1},{1,2},{2,3},{3,4},{4,5},{5,6},{6,7},{7,8},{8,9},{9,10},{10,1... | collective-permute-start | bytes 122888 | tf_op jit(solution)/shard_map/ppermute | solution.py:16
  108.7 0.3 collective-permute-done.6
  109.0 1.6 collective-permute-done.7
  110.6 0.7 select_maximum_fusion.4
  111.3 1.0 fusion.8
  112.4 0.1 fusion.65
  112.5 8.1 %collective-permute-start.8 = (f32[1,16,1024]{2,0,1:T(1,128)S(1)}, f32[1,16,1024]{2,0,1:T(1,128)S(1)}, u32[]{:S(2)}, u32[]{:S(2)}) collective-permute-start(f32[1,16,1024]{2,0,1:T(1,128)S(1)} %get-tuple-element.16), channel_id=1, source_target_pairs={{16,0},{32,16},{48,32},{64,48},{80,64},{96,80},{112,96},{128,112},... | collective-permute-start | bytes 196616 | tf_op jit(solution)/shard_map/ppermute | solution.py:19
  120.6 1.9 collective-permute-start.9
  122.5 25.1 %collective-permute-done.9 = f32[1,16,1024]{2,0,1:T(1,128)S(1)} collective-permute-done((f32[1,16,1024]{2,0,1:T(1,128)S(1)}, f32[1,16,1024]{2,0,1:T(1,128)S(1)}, u32[]{:S(2)}, u32[]{:S(2)}) %collective-permute-start.9) | collective-permute-done | bytes 65568 | tf_op jit(solution)/shard_map/ppermute | solution.py:16
  147.6 1.3 collective-permute-start.10
  148.9 7.7 %collective-permute-start.11 = (f32[10,1,1024]{2,0,1:T(8,128)S(1)}, f32[10,1,1024]{2,0,1:T(8,128)S(1)}, u32[]{:S(2)}, u32[]{:S(2)}) collective-permute-start(f32[10,1,1024]{2,0,1:T(8,128)S(1)} %get-tuple-element.9), channel_id=1, source_target_pairs={{0,1},{1,2},{2,3},{3,4},{4,5},{5,6},{6,7},{7,8},{8,9},{9,10},{10,1... | collective-permute-start | bytes 122888 | tf_op jit(solution)/shard_map/ppermute | solution.py:16
  156.7 0.4 collective-permute-done.10
  157.1 1.5 collective-permute-done.11
  158.5 0.7 select_maximum_fusion
  159.3 6.6 %multiply_reduce_fusion = (f32[8,1024]{1,0:T(8,128)S(1)}, f32[8,1024]{1,0:T(8,128)S(1)}, f32[8,1024]{1,0:T(8,128)S(1)}, f32[8,16,1024]{2,0,1:T(8,128)S(1)}) fusion(f32[8,16,1024]{2,0,1:T(8,128)S(1)} %fusion.8, f32[10,18,1026]{2,0,1:T(8,128)S(1)} %select_maximum_fusion, f32[1,16,1024]{2,0,1:T(1,128)S(1)} %collective-permute-done.8, ...), kind=kOutput, calls=%fused_computation.97 | output fusion | flops 7577600 | bytes 2981888 | tf_op jit(solution)/shard_map/jit(cumsum)/reduce_window_sum | solution.py:62
  165.9 0.1 stack.13
  166.0 0.1 stack.14
  166.1 0.1 stack.15
  166.3 0.1 exp.23
  166.4 0.2 constant_dynamic-slice_fusion.1
  166.7 4.3 %collective-permute-start.12 = (f32[4,8,2,2,2,64]{5,1,4,3,2,0:T(8,128)S(1)}, f32[4,8,2,2,2,64]{5,1,4,3,2,0:T(8,128)S(1)}, u32[]{:S(2)}, u32[]{:S(2)}) collective-permute-start(f32[4,8,2,2,2,64]{5,1,4,3,2,0:T(8,128)S(1)} %bitcast.82), channel_id=1, source_target_pairs={{0,1},{1,0},{2,3},{3,2},{4,5},{5,4},{6,7},{7,6},{8,9},{9,8},{10,11... | collective-permute-start | bytes 196616 | tf_op jit(solution)/shard_map/ppermute | solution.py:25
  171.0 2.9 %collective-permute-done.12 = f32[4,8,2,2,2,64]{5,1,4,3,2,0:T(8,128)S(1)} collective-permute-done((f32[4,8,2,2,2,64]{5,1,4,3,2,0:T(8,128)S(1)}, f32[4,8,2,2,2,64]{5,1,4,3,2,0:T(8,128)S(1)}, u32[]{:S(2)}, u32[]{:S(2)}) %collective-permute-start.12) | collective-permute-done | bytes 65568 | tf_op jit(solution)/shard_map/ppermute | solution.py:25
  174.0 5.4 %collective-permute-start.13 = (f32[4,8,2,2,64]{4,1,3,2,0:T(8,128)S(1)}, f32[4,8,2,2,64]{4,1,3,2,0:T(8,128)S(1)}, u32[]{:S(2)}, u32[]{:S(2)}) collective-permute-start(f32[4,8,2,2,64]{4,1,3,2,0:T(8,128)S(1)} %fusion.49), channel_id=1, source_target_pairs={{0,2},{1,3},{2,0},{3,1},{4,6},{5,7},{6,4},{7,5},{8,10},{9,11},{10,... | collective-permute-start | bytes 98312 | tf_op jit(solution)/shard_map/ppermute | solution.py:25
  179.4 2.2 %collective-permute-done.13 = f32[4,8,2,2,64]{4,1,3,2,0:T(8,128)S(1)} collective-permute-done((f32[4,8,2,2,64]{4,1,3,2,0:T(8,128)S(1)}, f32[4,8,2,2,64]{4,1,3,2,0:T(8,128)S(1)}, u32[]{:S(2)}, u32[]{:S(2)}) %collective-permute-start.13) | collective-permute-done | bytes 32800 | tf_op jit(solution)/shard_map/ppermute | solution.py:25
  181.7 7.4 %collective-permute-start.14 = (f32[4,8,2,64]{3,1,2,0:T(8,128)S(1)}, f32[4,8,2,64]{3,1,2,0:T(8,128)S(1)}, u32[]{:S(2)}, u32[]{:S(2)}) collective-permute-start(f32[4,8,2,64]{3,1,2,0:T(8,128)S(1)} %fusion.54), channel_id=1, source_target_pairs={{0,4},{1,5},{2,6},{3,7},{4,0},{5,1},{6,2},{7,3},{8,12},{9,13},{10,... | collective-permute-start | bytes 49160 | tf_op jit(solution)/shard_map/ppermute | solution.py:25
  189.1 2.3 %collective-permute-done.14 = f32[4,8,2,64]{3,1,2,0:T(8,128)S(1)} collective-permute-done((f32[4,8,2,64]{3,1,2,0:T(8,128)S(1)}, f32[4,8,2,64]{3,1,2,0:T(8,128)S(1)}, u32[]{:S(2)}, u32[]{:S(2)}) %collective-permute-start.14) | collective-permute-done | bytes 16416 | tf_op jit(solution)/shard_map/ppermute | solution.py:25
  191.5 6.8 %collective-permute-start.15 = (f32[4,8,64]{2,1,0:T(8,128)S(1)}, f32[4,8,64]{2,1,0:T(8,128)S(1)}, u32[]{:S(2)}, u32[]{:S(2)}) collective-permute-start(f32[4,8,64]{2,1,0:T(8,128)S(1)} %fusion.60), channel_id=1, source_target_pairs={{0,8},{1,9},{2,10},{3,11},{4,12},{5,13},{6,14},{7,15},{8,0},{9,1},... | collective-permute-start | bytes 24584 | tf_op jit(solution)/shard_map/ppermute | solution.py:25
  198.3 1.1 copy.42
  199.4 6.4 %collective-permute-done.15 = f32[4,8,64]{2,1,0:T(8,128)S(1)} collective-permute-done((f32[4,8,64]{2,1,0:T(8,128)S(1)}, f32[4,8,64]{2,1,0:T(8,128)S(1)}, u32[]{:S(2)}, u32[]{:S(2)}) %collective-permute-start.15) | collective-permute-done | bytes 8224 | tf_op jit(solution)/shard_map/ppermute | solution.py:25
  205.9 0.6 pad_maximum_fusion.33
  (32 shorter events, 0.4 us)
Async XLA Ops:
  0.6 66.4 %copy-start.1 = (bf16[3,8,16,1024]{3,2,1,0:T(8,128)(2,1)S(1)}, bf16[3,8,16,1024]{3,2,1,0:T(8,128)(2,1)}, u32[]{:S(2)}) copy-start(bf16[3,8,16,1024]{3,2,1,0:T(8,128)(2,1)} %param.5) | copy-start | bytes 2359300
  1.7 34.2 %collective-permute-start = (f32[1,16,1024]{2,0,1:T(1,128)S(1)}, f32[1,16,1024]{2,0,1:T(1,128)S(1)}, u32[]{:S(2)}, u32[]{:S(2)}) collective-permute-start(f32[1,16,1024]{2,0,1:T(1,128)S(1)} %copy.24), channel_id=1, source_target_pairs={{16,0},{32,16},{48,32},{64,48},{80,64},{96,80},{112,96},{128,112},... | collective-permute-start | bytes 196616 | tf_op jit(solution)/shard_map/ppermute | solution.py:19
  32.5 28.6 %collective-permute-start.1 = (f32[1,16,1024]{2,0,1:T(1,128)S(1)}, f32[1,16,1024]{2,0,1:T(1,128)S(1)}, u32[]{:S(2)}, u32[]{:S(2)}) collective-permute-start(f32[1,16,1024]{2,0,1:T(1,128)S(1)} %copy.26), channel_id=1, source_target_pairs={{0,16},{16,32},{32,48},{48,64},{64,80},{80,96},{96,112},{112,128},... | collective-permute-start | bytes 196616 | tf_op jit(solution)/shard_map/ppermute | solution.py:16
  61.2 6.4 %collective-permute-start.2 = (f32[10,1,1024]{2,0,1:T(8,128)S(1)}, f32[10,1,1024]{2,0,1:T(8,128)S(1)}, u32[]{:S(2)}, u32[]{:S(2)}) collective-permute-start(f32[10,1,1024]{2,0,1:T(8,128)S(1)} %get-tuple-element.14), channel_id=1, source_target_pairs={{1,0},{2,1},{3,2},{4,3},{5,4},{6,5},{7,6},{8,7},{9,8},{10,9},{11,1... | collective-permute-start | bytes 122888 | tf_op jit(solution)/shard_map/ppermute | solution.py:19
  62.5 6.4 %collective-permute-start.3 = (f32[10,1,1024]{2,0,1:T(8,128)S(1)}, f32[10,1,1024]{2,0,1:T(8,128)S(1)}, u32[]{:S(2)}, u32[]{:S(2)}) collective-permute-start(f32[10,1,1024]{2,0,1:T(8,128)S(1)} %get-tuple-element.13), channel_id=1, source_target_pairs={{0,1},{1,2},{2,3},{3,4},{4,5},{5,6},{6,7},{7,8},{8,9},{9,10},{10,1... | collective-permute-start | bytes 122888 | tf_op jit(solution)/shard_map/ppermute | solution.py:16
  67.5 2.1 %copy-start = (bf16[8,16,1024]{2,1,0:T(8,128)(2,1)S(1)}, bf16[8,16,1024]{2,1,0:T(8,128)(2,1)}, u32[]{:S(2)}) copy-start(bf16[8,16,1024]{2,1,0:T(8,128)(2,1)} %param.4) | copy-start | bytes 786436
  70.8 7.1 %collective-permute-start.4 = (f32[1,16,1024]{2,0,1:T(1,128)S(1)}, f32[1,16,1024]{2,0,1:T(1,128)S(1)}, u32[]{:S(2)}, u32[]{:S(2)}) collective-permute-start(f32[1,16,1024]{2,0,1:T(1,128)S(1)} %get-tuple-element.17), channel_id=1, source_target_pairs={{16,0},{32,16},{48,32},{64,48},{80,64},{96,80},{112,96},{128,112},... | collective-permute-start | bytes 196616 | tf_op jit(solution)/shard_map/ppermute | solution.py:19
  75.8 27.0 %collective-permute-start.5 = (f32[1,16,1024]{2,0,1:T(1,128)S(1)}, f32[1,16,1024]{2,0,1:T(1,128)S(1)}, u32[]{:S(2)}, u32[]{:S(2)}) collective-permute-start(f32[1,16,1024]{2,0,1:T(1,128)S(1)} %get-tuple-element.18), channel_id=1, source_target_pairs={{0,16},{16,32},{32,48},{48,64},{64,80},{80,96},{96,112},{112,128},... | collective-permute-start | bytes 196616 | tf_op jit(solution)/shard_map/ppermute | solution.py:16
  102.9 6.2 %collective-permute-start.6 = (f32[10,1,1024]{2,0,1:T(8,128)S(1)}, f32[10,1,1024]{2,0,1:T(8,128)S(1)}, u32[]{:S(2)}, u32[]{:S(2)}) collective-permute-start(f32[10,1,1024]{2,0,1:T(8,128)S(1)} %get-tuple-element.12), channel_id=1, source_target_pairs={{1,0},{2,1},{3,2},{4,3},{5,4},{6,5},{7,6},{8,7},{9,8},{10,9},{11,1... | collective-permute-start | bytes 122888 | tf_op jit(solution)/shard_map/ppermute | solution.py:19
  104.2 6.4 %collective-permute-start.7 = (f32[10,1,1024]{2,0,1:T(8,128)S(1)}, f32[10,1,1024]{2,0,1:T(8,128)S(1)}, u32[]{:S(2)}, u32[]{:S(2)}) collective-permute-start(f32[10,1,1024]{2,0,1:T(8,128)S(1)} %get-tuple-element.11), channel_id=1, source_target_pairs={{0,1},{1,2},{2,3},{3,4},{4,5},{5,6},{6,7},{7,8},{8,9},{9,10},{10,1... | collective-permute-start | bytes 122888 | tf_op jit(solution)/shard_map/ppermute | solution.py:16
  112.5 10.0 %collective-permute-start.8 = (f32[1,16,1024]{2,0,1:T(1,128)S(1)}, f32[1,16,1024]{2,0,1:T(1,128)S(1)}, u32[]{:S(2)}, u32[]{:S(2)}) collective-permute-start(f32[1,16,1024]{2,0,1:T(1,128)S(1)} %get-tuple-element.16), channel_id=1, source_target_pairs={{16,0},{32,16},{48,32},{64,48},{80,64},{96,80},{112,96},{128,112},... | collective-permute-start | bytes 196616 | tf_op jit(solution)/shard_map/ppermute | solution.py:19
  120.6 27.0 %collective-permute-start.9 = (f32[1,16,1024]{2,0,1:T(1,128)S(1)}, f32[1,16,1024]{2,0,1:T(1,128)S(1)}, u32[]{:S(2)}, u32[]{:S(2)}) collective-permute-start(f32[1,16,1024]{2,0,1:T(1,128)S(1)} %get-tuple-element.15), channel_id=1, source_target_pairs={{0,16},{16,32},{32,48},{48,64},{64,80},{80,96},{96,112},{112,128},... | collective-permute-start | bytes 196616 | tf_op jit(solution)/shard_map/ppermute | solution.py:16
  147.6 9.4 %collective-permute-start.10 = (f32[10,1,1024]{2,0,1:T(8,128)S(1)}, f32[10,1,1024]{2,0,1:T(8,128)S(1)}, u32[]{:S(2)}, u32[]{:S(2)}) collective-permute-start(f32[10,1,1024]{2,0,1:T(8,128)S(1)} %get-tuple-element.10), channel_id=1, source_target_pairs={{1,0},{2,1},{3,2},{4,3},{5,4},{6,5},{7,6},{8,7},{9,8},{10,9},{11,1... | collective-permute-start | bytes 122888 | tf_op jit(solution)/shard_map/ppermute | solution.py:19
  148.9 9.6 %collective-permute-start.11 = (f32[10,1,1024]{2,0,1:T(8,128)S(1)}, f32[10,1,1024]{2,0,1:T(8,128)S(1)}, u32[]{:S(2)}, u32[]{:S(2)}) collective-permute-start(f32[10,1,1024]{2,0,1:T(8,128)S(1)} %get-tuple-element.9), channel_id=1, source_target_pairs={{0,1},{1,2},{2,3},{3,4},{4,5},{5,6},{6,7},{7,8},{8,9},{9,10},{10,1... | collective-permute-start | bytes 122888 | tf_op jit(solution)/shard_map/ppermute | solution.py:16
  166.7 7.2 %collective-permute-start.12 = (f32[4,8,2,2,2,64]{5,1,4,3,2,0:T(8,128)S(1)}, f32[4,8,2,2,2,64]{5,1,4,3,2,0:T(8,128)S(1)}, u32[]{:S(2)}, u32[]{:S(2)}) collective-permute-start(f32[4,8,2,2,2,64]{5,1,4,3,2,0:T(8,128)S(1)} %bitcast.82), channel_id=1, source_target_pairs={{0,1},{1,0},{2,3},{3,2},{4,5},{5,4},{6,7},{7,6},{8,9},{9,8},{10,11... | collective-permute-start | bytes 196616 | tf_op jit(solution)/shard_map/ppermute | solution.py:25
  174.0 7.6 %collective-permute-start.13 = (f32[4,8,2,2,64]{4,1,3,2,0:T(8,128)S(1)}, f32[4,8,2,2,64]{4,1,3,2,0:T(8,128)S(1)}, u32[]{:S(2)}, u32[]{:S(2)}) collective-permute-start(f32[4,8,2,2,64]{4,1,3,2,0:T(8,128)S(1)} %fusion.49), channel_id=1, source_target_pairs={{0,2},{1,3},{2,0},{3,1},{4,6},{5,7},{6,4},{7,5},{8,10},{9,11},{10,... | collective-permute-start | bytes 98312 | tf_op jit(solution)/shard_map/ppermute | solution.py:25
  181.7 9.7 %collective-permute-start.14 = (f32[4,8,2,64]{3,1,2,0:T(8,128)S(1)}, f32[4,8,2,64]{3,1,2,0:T(8,128)S(1)}, u32[]{:S(2)}, u32[]{:S(2)}) collective-permute-start(f32[4,8,2,64]{3,1,2,0:T(8,128)S(1)} %fusion.54), channel_id=1, source_target_pairs={{0,4},{1,5},{2,6},{3,7},{4,0},{5,1},{6,2},{7,3},{8,12},{9,13},{10,... | collective-permute-start | bytes 49160 | tf_op jit(solution)/shard_map/ppermute | solution.py:25
  191.5 14.3 %collective-permute-start.15 = (f32[4,8,64]{2,1,0:T(8,128)S(1)}, f32[4,8,64]{2,1,0:T(8,128)S(1)}, u32[]{:S(2)}, u32[]{:S(2)}) collective-permute-start(f32[4,8,64]{2,1,0:T(8,128)S(1)} %fusion.60), channel_id=1, source_target_pairs={{0,8},{1,9},{2,10},{3,11},{4,12},{5,13},{6,14},{7,15},{8,0},{9,1},... | collective-permute-start | bytes 24584 | tf_op jit(solution)/shard_map/ppermute | solution.py:25
where the time goes:
time: 208 us; the launch traced here: 206 us
  waiting for transfers between devices  94.4 us (45%)
  starting transfers between devices  94.2 us (45%)
  other arithmetic  12.2 us (6%)
  local copies, waits for them, and re-layouts  4.44 us (2%)
    ppermute x6, waiting for transfers between devices, extended_2(): lax.ppermute(lax.slice_in_dim(block, block.shape[dim] - width, None, axis...  79.8 us
    ppermute x6, starting transfers between devices, extended_2(): lax.ppermute(lax.slice_in_dim(block, 0, width, axis=dim), axis, backward)  47.7 us
    ppermute x4, starting transfers between devices, swapped(): lax.ppermute(value, axis, [(i, i ^ 1 << apart) for i in range(lax.axis_si...  23.9 us
    ppermute x6, starting transfers between devices, extended_2(): lax.ppermute(lax.slice_in_dim(block, block.shape[dim] - width, None, axis...  22.6 us
    ppermute x4, waiting for transfers between devices, swapped(): lax.ppermute(value, axis, [(i, i ^ 1 << apart) for i in range(lax.axis_si...  13.7 us
    another operation x1, other arithmetic, render(): through = jnp.cumsum(optical, axis=1)  6.65 us
  transfers between devices with their start and end apart: 16, of which 13 were waited for; matrix products, arithmetic and copies ran while one was open for 1% of the time, Pallas kernels for 0%

commit v1 on v0

v1 whole, which is shorter than its diff:
```python
import functools

import jax
import jax.numpy as jnp
from jax import lax
from jax.experimental import pallas as pl
from jax.experimental.pallas import tpu as pltpu
from jax.sharding import PartitionSpec as P

TIME_STEP = 0.2
OPACITY_TOTAL = 3.0
MESH = pl.DeviceIdType.MESH

(FAR_U, FAR_C, NEAR_U, LO_U, HI_U, NEAR_M, LO_M, HI_M, NEAR_F, FAR_M,
 LO_MB, HI_MB, FAR_P, LO_F, HI_F, LO_FB, HI_FB, COPIES) = range(18)


def shifted(value, before, axis, low, high):
    size = value.shape[axis]
    index = lax.broadcasted_iota(jnp.int32, value.shape, axis)
    if before:
        return jnp.where(index == 0, low, pltpu.roll(value, 1, axis))
    return jnp.where(index == size - 1, high, pltpu.roll(value, size - 1, axis))


def section(ref, low, high, diff, vel, i):
    center, row_before, row_after = ref[i + 1], ref[i], ref[i + 2]
    deep_before = shifted(center, True, 0, low[i], None)
    deep_after = shifted(center, False, 0, None, high[i])
    col_before = shifted(center, True, 1, 0.0, None)
    col_after = shifted(center, False, 1, None, 0.0)
    k = diff[i].astype(jnp.float32)
    total = 1.0 - 6.0 * k
    flow = None
    for dim, (back, ahead) in enumerate(
        ((row_before, row_after), (deep_before, deep_after), (col_before, col_after))
    ):
        speed = vel[dim, i].astype(jnp.float32)
        up, down = jnp.maximum(speed, 0.0), jnp.minimum(speed, 0.0)
        part = (k + up) * back + (k - down) * ahead
        flow = part if flow is None else flow + part
        total = total - (up - down)
    return center + TIME_STEP * (flow + center * (total - center))


def ray_row(ref, low, high, i, opacity):
    center = ref[i + 1]
    grad_row = (ref[i + 2] - ref[i]) * 0.5
    grad_deep = (shifted(center, False, 0, None, high[i]) - shifted(center, True, 0, low[i], None)) * 0.5
    grad_col = (shifted(center, False, 1, None, 0.0) - shifted(center, True, 1, 0.0, None)) * 0.5
    lighting = 0.48 * grad_row + 0.64 * grad_deep + 0.6 * grad_col
    magnitude = grad_row * grad_row + grad_deep * grad_deep + grad_col * grad_col + 0.1
    shade = 0.35 + 0.65 * lighting * lighting / magnitude
    optical = opacity * center
    size = center.shape[0]
    index = lax.broadcasted_iota(jnp.int32, center.shape, 0)
    through, step = optical, 1
    while step < size:
        through = through + jnp.where(index >= step, pltpu.roll(through, step, 0), 0.0)
        step *= 2
    weight = jnp.exp(optical - through) * (1.0 - jnp.exp(-optical)) * shade
    bright = weight * center
    red = jnp.sum(bright, axis=0, keepdims=True)
    green = jnp.sum(bright * center, axis=0, keepdims=True)
    blue = jnp.sum(weight - bright, axis=0, keepdims=True)
    return red, green, blue, jnp.exp(-through[size - 1 : size])


def kernel(rows, depths, opacity, field, diffusivity, velocity, front_out, picture, u, m, f, diff,
           vel, coef, far_u, far_c, far_m, far_p, p_row, lo, hi, edge_lo, edge_hi, lo_b, hi_b,
           edge_lo_b, edge_hi_b, part, comp, result, load, store, send, recv, send_a, recv_a):
    r, d = lax.axis_index("rows"), lax.axis_index("depth")
    core = r % 2
    count = field.shape[0]
    last = count - 1
    b = last * core
    inner = last - 1 - (last - 2) * (1 - core)
    near_row = last - b
    far_slot = (count + 1) * core
    first_free = 2 * (1 - core)
    near, far = r + 1 - 2 * core, r - 1 + 2 * core
    has_far = jnp.logical_and(far >= 0, far < rows)
    has_lo, has_hi = d > 0, d < depths - 1
    tiles = field.shape[2] // 128

    loads = [
        pltpu.make_async_copy(field, u.at[pl.ds(1, count)], load.at[0]),
        pltpu.make_async_copy(diffusivity, diff, load.at[1]),
        pltpu.make_async_copy(velocity, vel, load.at[2]),
    ]
    barrier = pltpu.get_barrier_semaphore()

    @pl.when(has_far)
    def _():
        pl.semaphore_signal(barrier, inc=1, device_id=(far, d), device_id_type=MESH)

    pl.semaphore_signal(barrier, inc=1, device_id=(near, d), device_id_type=MESH)

    def greet(k, carry):
        pl.semaphore_signal(
            barrier, inc=1, device_id=(r, lax.rem(d + k, depths)), device_id_type=MESH
        )
        return carry

    for copy in loads:
        copy.start()
    lax.fori_loop(1, depths, greet, 0)

    zero_row = jnp.zeros(u.shape[1:], jnp.float32)
    u[far_slot] = zero_row
    m[far_slot] = zero_row

    @pl.when(jnp.logical_not(has_far))
    def _():
        for ref in (far_u, far_c, far_m, far_p):
            ref[...] = zero_row

    @pl.when(jnp.logical_not(has_lo))
    def _():
        lo[...] = jnp.zeros_like(lo)
        lo_b[...] = jnp.zeros_like(lo_b)

    @pl.when(jnp.logical_not(has_hi))
    def _():
        hi[...] = jnp.zeros_like(hi)
        hi_b[...] = jnp.zeros_like(hi_b)

    for copy in loads:
        copy.wait()

    k = diff[b].astype(jnp.float32)
    speed = vel[0, b].astype(jnp.float32)
    coef[...] = TIME_STEP * (
        k + jnp.where(core == 1, -jnp.minimum(speed, 0.0), jnp.maximum(speed, 0.0))
    )

    def edges(i, stage, value):
        edge_lo[stage, i] = value[:1]
        edge_hi[stage, i] = value[-1:]

    def field_edges(i, carry):
        edges(i, 0, u[i + 1])
        return carry

    lax.fori_loop(0, count, field_edges, 0)

    pl.semaphore_wait(barrier, depths + has_far.astype(jnp.int32))

    def remote(name, src, dst, target):
        return pltpu.make_async_remote_copy(
            src_ref=src, dst_ref=dst, send_sem=send.at[name], recv_sem=recv.at[name],
            device_id=target, device_id_type=MESH,
        )

    far_copies = {
        FAR_U: remote(FAR_U, u.at[b + 1], far_u, (far, d)),
        FAR_C: remote(FAR_C, coef, far_c, (far, d)),
        FAR_M: remote(FAR_M, m.at[b + 1], far_m, (far, d)),
        FAR_P: remote(FAR_P, p_row, far_p, (far, d)),
    }
    near_slot = (count + 1) * core
    near_copies = {
        name: remote(name, ref.at[near_row + 1], ref.at[near_slot], (near, d))
        for name, ref in ((NEAR_U, u), (NEAR_M, m), (NEAR_F, f))
    }
    lo_copies = {
        name: remote(name, src, dst, (r, d - 1))
        for name, src, dst in (
            (LO_U, edge_lo.at[0], hi.at[0]), (LO_M, edge_lo.at[1], hi.at[1]),
            (LO_F, edge_lo.at[2], hi.at[2]), (LO_MB, edge_lo_b.at[0], hi_b.at[0]),
            (LO_FB, edge_lo_b.at[1], hi_b.at[1]),
        )
    }
    hi_copies = {
        name: remote(name, src, dst, (r, d + 1))
        for name, src, dst in (
            (HI_U, edge_hi.at[0], lo.at[0]), (HI_M, edge_hi.at[1], lo.at[1]),
            (HI_F, edge_hi.at[2], lo.at[2]), (HI_MB, edge_hi_b.at[0], lo_b.at[0]),
            (HI_FB, edge_hi_b.at[1], lo_b.at[1]),
        )
    }

    def send_deep(to_lo, to_hi):
        @pl.when(has_lo)
        def _():
            lo_copies[to_lo].start()

        @pl.when(has_hi)
        def _():
            hi_copies[to_hi].start()

    def wait_deep(to_lo, to_hi):
        @pl.when(has_hi)
        def _():
            lo_copies[to_lo].wait_recv()

        @pl.when(has_lo)
        def _():
            hi_copies[to_hi].wait_recv()

    @pl.when(has_far)
    def _():
        far_copies[FAR_U].start()

    near_copies[NEAR_U].start()
    send_deep(LO_U, HI_U)

    @pl.when(has_far)
    def _():
        far_copies[FAR_C].start()

    near_copies[NEAR_U].wait_recv()
    wait_deep(LO_U, HI_U)

    def first(i, carry):
        value = section(u, lo.at[0], hi.at[0], diff, vel, i)
        m[i + 1] = value
        edges(i, 1, value)
        return carry

    lax.fori_loop(0, count, first, 0)
    near_copies[NEAR_M].start()
    send_deep(LO_M, HI_M)
    near_copies[NEAR_M].wait_recv()
    wait_deep(LO_M, HI_M)

    def second(i, carry):
        value = section(m, lo.at[1], hi.at[1], diff, vel, i)
        f[i + 1] = value
        edges(i, 2, value)
        return carry

    lax.fori_loop(first_free, first_free + count - 2, second, 0)
    near_copies[NEAR_F].start()

    @pl.when(has_far)
    def _():
        far_copies[FAR_U].wait_recv()

    value = m[b + 1] + coef[...] * far_u[...]
    m[b + 1] = value
    edge_lo_b[0] = value[:1]
    edge_hi_b[0] = value[-1:]
    send_deep(LO_MB, HI_MB)

    @pl.when(has_far)
    def _():
        far_copies[FAR_M].start()

    wait_deep(LO_MB, HI_MB)
    lo[1, b] = lo_b[0]
    hi[1, b] = hi_b[0]
    value = section(m, lo.at[1], hi.at[1], diff, vel, b)
    p_row[...] = value

    @pl.when(has_far)
    def _():
        far_copies[FAR_P].start()

    edges(b, 2, value)
    second(inner, 0)
    send_deep(LO_F, HI_F)
    near_copies[NEAR_F].wait_recv()
    wait_deep(LO_F, HI_F)

    def pair(p, carry):
        low, high = lo.at[2], hi.at[2]
        one = ray_row(f, low, high, 2 * p, opacity)
        two = ray_row(f, low, high, 2 * p + 1, opacity)
        both = jnp.concatenate([x for v in zip(one, two) for x in v], axis=0)
        for j in range(tiles):
            part[j, p] = both[:, j * 128 : (j + 1) * 128]
        return carry

    pairs = count // 2
    early = pl.ds(1 - core, pairs - 1)
    late_pair = (pairs - 1) * core
    lax.fori_loop(1 - core, pairs - core, pair, 0)

    def spread(stage, span, k):
        target = lax.rem(d + k, depths)
        return pltpu.make_async_remote_copy(
            src_ref=part.at[target // 2, span], dst_ref=comp.at[d, span],
            send_sem=send_a.at[stage, k], recv_sem=recv_a.at[stage, d],
            device_id=(r, target), device_id_type=MESH,
        )

    def arrived(stage, span, k):
        source = lax.rem(d + k, depths)
        pltpu.make_async_remote_copy(
            src_ref=part.at[0, span], dst_ref=comp.at[source, span],
            send_sem=send_a.at[stage, k], recv_sem=recv_a.at[stage, source],
            device_id=(r, source), device_id_type=MESH,
        ).wait_recv()

    def start_spread(stage, span):
        def body(k, carry):
            spread(stage, span, k).start()
            return carry

        lax.fori_loop(1, depths, body, 0)

    def end_spread(stage, span):
        def body(k, carry):
            arrived(stage, span, k)
            return carry

        lax.fori_loop(1, depths, body, 0)

    start_spread(0, early)

    @pl.when(has_far)
    def _():
        far_copies[FAR_M].wait_recv()

    value = p_row[...] + coef[...] * far_m[...]
    f[b + 1] = value
    edge_lo_b[1] = value[:1]
    edge_hi_b[1] = value[-1:]
    send_deep(LO_FB, HI_FB)
    write = pltpu.make_async_copy(f.at[pl.ds(1, count)], front_out, store.at[0])
    write.start()

    @pl.when(has_far)
    def _():
        far_copies[FAR_C].wait_recv()
        far_copies[FAR_P].wait_recv()

    f[far_slot] = far_p[...] + far_c[...] * m[b + 1]
    wait_deep(LO_FB, HI_FB)
    lo[2, b] = lo_b[1]
    hi[2, b] = hi_b[1]
    pair(late_pair, 0)
    late = pl.ds(late_pair, 1)
    start_spread(1, late)
    for p in range(pairs):
        comp[d, p] = part[d // 2, p]

    def composite(p, carry):
        total = jnp.zeros((6, 128), jnp.float32)
        clear = jnp.ones((2, 128), jnp.float32)
        for s in range(depths):
            block = comp[s, p]
            total = total + jnp.concatenate([clear] * 3, axis=0) * block[:6]
            clear = clear * block[6:]
        tile = jnp.concatenate([total, clear], axis=0)
        result[p] = jnp.where(d % 2 == 0, tile, pltpu.roll(tile, 64, 1))
        return carry

    end_spread(0, early)
    lax.fori_loop(1 - core, pairs - core, composite, 0)
    end_spread(1, late)
    composite(late_pair, 0)
    for p in range(pairs):
        tile = result[p]
        for v in range(4):
            picture[v, 2 * p : 2 * p + 2] = tile[2 * v : 2 * v + 2, : picture.shape[2]]

    for name in near_copies:
        near_copies[name].wait_send()

    @pl.when(has_far)
    def _():
        for name in far_copies:
            far_copies[name].wait_send()

    @pl.when(has_lo)
    def _():
        for name in lo_copies:
            lo_copies[name].wait_send()

    @pl.when(has_hi)
    def _():
        for name in hi_copies:
            hi_copies[name].wait_send()

    def sent(k, carry):
        spread(0, early, k).wait_send()
        spread(1, late, k).wait_send()
        return carry

    lax.fori_loop(1, depths, sent, 0)
    write.wait()


def shards(rows, depths, field, diffusivity, velocity):
    count, deep, width = field.shape
    row = (deep, width)
    f32 = jnp.float32
    tiles, pairs = width // 128, count // 2
    any_space = pl.BlockSpec(memory_space=pl.ANY)
    vmem = pltpu.VMEM
    return pl.pallas_call(
        functools.partial(kernel, rows, depths, OPACITY_TOTAL / (deep * depths)),
        out_shape=(
            jax.ShapeDtypeStruct(field.shape, f32),
            jax.ShapeDtypeStruct((4, count, width // depths), f32),
        ),
        in_specs=[any_space] * 3,
        out_specs=(any_space, pl.BlockSpec(memory_space=pltpu.VMEM)),
        scratch_shapes=[
            vmem((count + 2,) + row, f32),
            vmem((count + 2,) + row, f32),
            vmem((count + 2,) + row, f32),
            vmem(diffusivity.shape, diffusivity.dtype),
            vmem(velocity.shape, velocity.dtype),
            vmem(row, f32), vmem(row, f32), vmem(row, f32), vmem(row, f32), vmem(row, f32), vmem(row, f32),
            vmem((3, count, 1, width), f32), vmem((3, count, 1, width), f32),
            vmem((3, count, 1, width), f32), vmem((3, count, 1, width), f32),
            vmem((2, 1, width), f32), vmem((2, 1, width), f32),
            vmem((2, 1, width), f32), vmem((2, 1, width), f32),
            vmem((tiles, pairs, 8, 128), f32),
            vmem((depths, pairs, 8, 128), f32),
            vmem((pairs, 8, 128), f32),
            pltpu.SemaphoreType.DMA((3,)),
            pltpu.SemaphoreType.DMA((1,)),
            pltpu.SemaphoreType.DMA((COPIES,)),
            pltpu.SemaphoreType.DMA((COPIES,)),
            pltpu.SemaphoreType.DMA((2, depths)),
            pltpu.SemaphoreType.DMA((2, depths)),
        ],
        compiler_params=pltpu.CompilerParams(collective_id=0, has_side_effects=True),
        name="front_and_rays",
    )(field, diffusivity, velocity)


def solution(mesh):
    return jax.shard_map(
        functools.partial(shards, mesh.shape["rows"], mesh.shape["depth"]),
        mesh=mesh,
        in_specs=(
            P("rows", "depth", None),
            P("rows", "depth", None),
            P(None, "rows", "depth", None),
        ),
        out_specs=(P("rows", "depth", None), P(None, "rows", "depth")),
        check_vma=False,
    )
```

time: 208 us -> 117 us (0.56)
  the two profiles are of different devices: /device:TPU:24 before, /device:TPU:4 now
where the time goes in v1:
time: 117 us
  Pallas kernels  113 us (97%)
  local copies, waits for them, and re-layouts  2.5 us (2%)
    pallas_call x1, Pallas kernels, shards(): pl.pallas_call(functools.partial(kernel, rows, depths, OPACITY_TOTAL / (d...  113 us
    unnamed x4, local copies, waits for them, and re-layouts  2.5 us

profile of v1, /device:TPU:4, one launch (start us, length us, event | category | flops | bytes accessed | tf_op | source)
XLA Modules:
  0.0 116.6 jit_solution(11328290552301049991)
XLA Ops:
  0.6 113.5 %front_and_rays.1 = (f32[8,16,1024]{2,1,0:T(8,128)}, f32[4,8,64]{2,1,0:T(8,128)}) custom-call(f32[8,16,1024]{2,1,0:T(8,128)} %field.1, bf16[8,16,1024]{2,1,0:T(8,128)(2,1)} %diffusivity.1, bf16[3,8,16,1024]{3,2,1,0:T(8,128)(2,1)} %velocity.1), custom_call_target="tpu_custom_call" | custom-call | tf_op jit(solution)/shard_map/front_and_rays/pallas_call | solution.py:393
  114.1 0.0 copy-start
  114.1 1.9 %copy.7 = f32[8,16,1024]{2,1,0:T(8,128)} copy(f32[8,16,1024]{2,1,0:T(8,128)} %get-tuple-element.4) | data formatting | bytes 1048576
  116.0 0.0 copy-done
  116.0 0.6 copy.8
Async XLA Ops:
  114.1 1.9 %copy-start = (f32[4,8,64]{2,1,0:T(8,128)S(1)}, f32[4,8,64]{2,1,0:T(8,128)}, u32[]{:S(2)}) copy-start(f32[4,8,64]{2,1,0:T(8,128)} %get-tuple-element.5) | copy-start | bytes 24580

commit v2 on v1

v2 whole, which is shorter than its diff:
```python
import functools

import jax
import jax.numpy as jnp
from jax import lax
from jax.experimental import pallas as pl
from jax.experimental.pallas import tpu as pltpu
from jax.sharding import PartitionSpec as P

TIME_STEP = 0.2
OPACITY_TOTAL = 3.0
MESH = pl.DeviceIdType.MESH

(NEAR_U, LO_U, HI_U, NEAR_M, LO_M, HI_M, NEAR_F, LO_F, HI_F,
 LO_MB, HI_MB, LO_FB, HI_FB, FAR_U) = range(14)
SPLIT = 2
CHUNKS = 2 * SPLIT
FAR_M, FAR_F = FAR_U + CHUNKS, FAR_U + 2 * CHUNKS
COPIES = FAR_U + 3 * CHUNKS


def shifted(value, before, axis, low, high):
    size = value.shape[axis]
    index = lax.broadcasted_iota(jnp.int32, value.shape, axis)
    if before:
        return jnp.where(index == 0, low, pltpu.roll(value, 1, axis))
    return jnp.where(index == size - 1, high, pltpu.roll(value, size - 1, axis))


def section(ref, low, high, diff, vel, i):
    center, row_before, row_after = ref[i + 1], ref[i], ref[i + 2]
    deep_before = shifted(center, True, 0, low[i], None)
    deep_after = shifted(center, False, 0, None, high[i])
    col_before = shifted(center, True, 1, 0.0, None)
    col_after = shifted(center, False, 1, None, 0.0)
    k = diff[i].astype(jnp.float32)
    total = 1.0 - 6.0 * k
    flow = None
    for dim, (back, ahead) in enumerate(
        ((row_before, row_after), (deep_before, deep_after), (col_before, col_after))
    ):
        speed = vel[dim, i].astype(jnp.float32)
        up, down = jnp.maximum(speed, 0.0), jnp.minimum(speed, 0.0)
        part = (k + up) * back + (k - down) * ahead
        flow = part if flow is None else flow + part
        total = total - (up - down)
    return center + TIME_STEP * (flow + center * (total - center))


def ray_row(ref, low, high, i, opacity):
    center = ref[i + 1]
    grad_row = (ref[i + 2] - ref[i]) * 0.5
    grad_deep = (shifted(center, False, 0, None, high[i]) - shifted(center, True, 0, low[i], None)) * 0.5
    grad_col = (shifted(center, False, 1, None, 0.0) - shifted(center, True, 1, 0.0, None)) * 0.5
    lighting = 0.48 * grad_row + 0.64 * grad_deep + 0.6 * grad_col
    magnitude = grad_row * grad_row + grad_deep * grad_deep + grad_col * grad_col + 0.1
    shade = 0.35 + 0.65 * lighting * lighting / magnitude
    optical = opacity * center
    size = center.shape[0]
    index = lax.broadcasted_iota(jnp.int32, center.shape, 0)
    through, step = optical, 1
    while step < size:
        through = through + jnp.where(index >= step, pltpu.roll(through, step, 0), 0.0)
        step *= 2
    weight = jnp.exp(optical - through) * (1.0 - jnp.exp(-optical)) * shade
    bright = weight * center
    red = jnp.sum(bright, axis=0, keepdims=True)
    green = jnp.sum(bright * center, axis=0, keepdims=True)
    blue = jnp.sum(weight - bright, axis=0, keepdims=True)
    return red, green, blue, jnp.exp(-through[size - 1 : size])


def kernel(rows, depths, opacity, field, diffusivity, velocity, front_out, picture, u, m, f, diff,
           vel, coef, far_u, far_m, p_row, lo, hi, edge_lo, edge_hi, lo_b, hi_b,
           edge_lo_b, edge_hi_b, part, comp, result, load, store, send, recv, send_a, recv_a, token):
    r, d = lax.axis_index("rows"), lax.axis_index("depth")
    core = r % 2
    count = field.shape[0]
    last = count - 1
    b = last * core
    inner = last - 1 - (last - 2) * (1 - core)
    near_row = last - b
    far_slot = (count + 1) * core
    first_free = 2 * (1 - core)
    near, far = r + 1 - 2 * core, r - 1 + 2 * core
    has_far = jnp.logical_and(far >= 0, far < rows)
    has_lo, has_hi = d > 0, d < depths - 1
    upper = r // 2 % 2 == 1
    tiles = field.shape[2] // 128

    loads = [
        pltpu.make_async_copy(field, u.at[pl.ds(1, count)], load.at[0]),
        pltpu.make_async_copy(diffusivity, diff, load.at[1]),
        pltpu.make_async_copy(velocity, vel, load.at[2]),
    ]
    barrier = pltpu.get_barrier_semaphore()

    @pl.when(has_far)
    def _():
        pl.semaphore_signal(barrier, inc=1, device_id=(far, d), device_id_type=MESH)

    pl.semaphore_signal(barrier, inc=1, device_id=(near, d), device_id_type=MESH)

    for there, target in ((has_lo, d - 1), (has_hi, d + 1)):
        @pl.when(there)
        def _():
            pl.semaphore_signal(barrier, inc=1, device_id=(r, target), device_id_type=MESH)

    for copy in loads:
        copy.start()

    zero_row = jnp.zeros(u.shape[1:], jnp.float32)
    u[far_slot] = zero_row
    m[far_slot] = zero_row

    @pl.when(jnp.logical_not(has_far))
    def _():
        far_u[...] = zero_row
        far_m[...] = zero_row
        f[far_slot] = zero_row

    @pl.when(jnp.logical_not(has_lo))
    def _():
        lo[...] = jnp.zeros_like(lo)
        lo_b[...] = jnp.zeros_like(lo_b)

    @pl.when(jnp.logical_not(has_hi))
    def _():
        hi[...] = jnp.zeros_like(hi)
        hi_b[...] = jnp.zeros_like(hi_b)

    for copy in loads:
        copy.wait()

    k = diff[b].astype(jnp.float32)
    speed = vel[0, b].astype(jnp.float32)
    coef[...] = TIME_STEP * (
        k + jnp.where(core == 1, -jnp.minimum(speed, 0.0), jnp.maximum(speed, 0.0))
    )

    def edges(i, stage, value):
        edge_lo[stage, i] = value[:1]
        edge_hi[stage, i] = value[-1:]

    def field_edges(i, carry):
        edges(i, 0, u[i + 1])
        return carry

    lax.fori_loop(0, count, field_edges, 0)

    pl.semaphore_wait(barrier, 1 + sum(x.astype(jnp.int32) for x in (has_far, has_lo, has_hi)))

    def remote(name, src, dst, target):
        return pltpu.make_async_remote_copy(
            src_ref=src, dst_ref=dst, send_sem=send.at[name], recv_sem=recv.at[name],
            device_id=target, device_id_type=MESH,
        )

    deep, wide = u.shape[1] // 2, u.shape[2] // SPLIT
    chunk = [
        (pl.ds(deep * p, deep), pl.ds(wide * q, wide)) for q in range(SPLIT) for p in range(2)
    ]
    far_copies = {}
    for h, at in enumerate(chunk):
        for name, src, dst in (
            (FAR_U, u.at[(b + 1,) + at], far_u.at[at]),
            (FAR_M, m.at[(b + 1,) + at], far_m.at[at]),
            (FAR_F, f.at[(b + 1,) + at], f.at[((count + 1) * (1 - core),) + at]),
        ):
            far_copies[name + h] = remote(name + h, src, dst, (far, d))
    near_slot = (count + 1) * core
    near_copies = {
        name: remote(name, ref.at[near_row + 1], ref.at[near_slot], (near, d))
        for name, ref in ((NEAR_U, u), (NEAR_M, m), (NEAR_F, f))
    }
    lo_copies = {
        name: remote(name, src, dst, (r, d - 1))
        for name, src, dst in (
            (LO_U, edge_lo.at[0], hi.at[0]), (LO_M, edge_lo.at[1], hi.at[1]),
            (LO_F, edge_lo.at[2], hi.at[2]), (LO_MB, edge_lo_b.at[0, 0], hi_b.at[0, 0]),
            (LO_FB, edge_lo_b.at[1], hi_b.at[1]),
        )
    }
    hi_copies = {
        name: remote(name, src, dst, (r, d + 1))
        for name, src, dst in (
            (HI_U, edge_hi.at[0], lo.at[0]), (HI_M, edge_hi.at[1], lo.at[1]),
            (HI_F, edge_hi.at[2], lo.at[2]), (HI_MB, edge_hi_b.at[0, 0], lo_b.at[0, 0]),
            (HI_FB, edge_hi_b.at[1], lo_b.at[1]),
        )
    }

    started = {}

    def start_far(name):
        started[name] = far_copies[name], has_far

        @pl.when(has_far)
        def _():
            far_copies[name].start()

    def wait_far(name):
        @pl.when(has_far)
        def _():
            far_copies[name].wait_recv()

    def start_near(name):
        started[name] = near_copies[name], None
        near_copies[name].start()

    def wait_near(name):
        near_copies[name].wait_recv()

    def start_deep(to_lo=None, to_hi=None):
        if to_lo is not None:
            started[to_lo] = lo_copies[to_lo], has_lo
            pl.when(has_lo)(lo_copies[to_lo].start)
        if to_hi is not None:
            started[to_hi] = hi_copies[to_hi], has_hi
            pl.when(has_hi)(hi_copies[to_hi].start)

    def wait_deep(to_lo, to_hi):
        pl.when(has_hi)(lo_copies[to_lo].wait_recv)
        pl.when(has_lo)(hi_copies[to_hi].wait_recv)

    start_deep(LO_U, HI_U)
    start_near(NEAR_U)
    for h in range(CHUNKS):
        start_far(FAR_U + h)
    wait_near(NEAR_U)
    wait_deep(LO_U, HI_U)

    def first(i, carry):
        value = section(u, lo.at[0], hi.at[0], diff, vel, i)
        m[i + 1] = value
        edges(i, 1, value)
        return carry

    lax.fori_loop(0, count, first, 0)
    start_deep(LO_M, HI_M)
    start_near(NEAR_M)
    wait_near(NEAR_M)
    wait_deep(LO_M, HI_M)

    def line_entered():
        for way, there, on, onward in ((0, has_lo, has_hi, d + 1), (1, has_hi, has_lo, d - 1)):
            @pl.when(there)
            def _():
                pl.semaphore_wait(token.at[way], 1)

            @pl.when(on)
            def _():
                pl.semaphore_signal(
                    token.at[way], inc=1, device_id=(r, onward), device_id_type=MESH
                )

    pl.when(upper)(line_entered)

    for h, at in enumerate(chunk):
        wait_far(FAR_U + h)
        here = (b + 1,) + at
        m[here] = m[here] + coef[at] * far_u[at]
        if h == CHUNKS - 1:
            edge_lo_b[0, 0] = m[b + 1, :1]
            edge_hi_b[0, 0] = m[b + 1, u.shape[1] - 1 :]
            start_deep(LO_MB, HI_MB)
        start_far(FAR_M + h)
    wait_deep(LO_MB, HI_MB)
    lo[1, b] = lo_b[0, 0]
    hi[1, b] = hi_b[0, 0]
    p_row[...] = section(m, lo.at[1], hi.at[1], diff, vel, b)

    def second(i, carry):
        value = section(m, lo.at[1], hi.at[1], diff, vel, i)
        f[i + 1] = value
        edges(i, 2, value)
        return carry

    def pair(p, carry):
        low, high = lo.at[2], hi.at[2]
        one, two = (
            jnp.concatenate(ray_row(f, low, high, 2 * p + q, opacity), axis=0) for q in range(2)
        )
        left = lax.broadcasted_iota(jnp.int32, (4, 128), 1) < 64
        for j in range(tiles):
            x, y = one[:, j * 128 : (j + 1) * 128], two[:, j * 128 : (j + 1) * 128]
            part[2 * j, p] = jnp.where(left, x, pltpu.roll(y, 64, 1))
            part[2 * j + 1, p] = jnp.where(left, pltpu.roll(x, 64, 1), y)
        return carry

    pairs = count // 2
    groups = pl.ds(1 - core, pairs - 1), pl.ds((pairs - 1) * core, 1)

    def spread(stage, k):
        target = lax.rem(d + k, depths)
        return pltpu.make_async_remote_copy(
            src_ref=part.at[target, groups[stage]], dst_ref=comp.at[d, groups[stage]],
            send_sem=send_a.at[stage, k], recv_sem=recv_a.at[stage, d],
            device_id=(r, target), device_id_type=MESH,
        )

    def start_spread(stage):
        def body(k, carry):
            spread(stage, k).start()
            return carry

        lax.fori_loop(1, depths, body, 0)

    def end_spread(stage):
        def body(k, carry):
            source = lax.rem(d + k, depths)
            pltpu.make_async_remote_copy(
                src_ref=part.at[0, groups[stage]], dst_ref=comp.at[source, groups[stage]],
                send_sem=send_a.at[stage, k], recv_sem=recv_a.at[stage, source],
                device_id=(r, source), device_id_type=MESH,
            ).wait_recv()
            return carry

        lax.fori_loop(1, depths, body, 0)

    def early_images():
        lax.fori_loop(first_free, first_free + count - 2, second, 0)
        start_deep(LO_F, HI_F)
        start_near(NEAR_F)
        value = section(m, lo.at[1], hi.at[1], diff, vel, inner)
        f[inner + 1] = value
        edge_lo_b[1, 1] = value[:1]
        edge_hi_b[1, 1] = value[-1:]
        pl.when(jnp.logical_not(upper))(line_entered)
        wait_near(NEAR_F)
        wait_deep(LO_F, HI_F)
        lax.fori_loop(1 - core, pairs - core, pair, 0)
        start_spread(0)

    pl.when(jnp.logical_not(upper))(early_images)
    for h, at in enumerate(chunk):
        wait_far(FAR_M + h)
        f[(b + 1,) + at] = p_row[at] + coef[at] * far_m[at]
        start_far(FAR_F + h)
    pl.when(upper)(early_images)
    edge_lo_b[1, 0] = f[b + 1, :1]
    edge_hi_b[1, 0] = f[b + 1, u.shape[1] - 1 :]
    start_deep(LO_FB, HI_FB)
    write = pltpu.make_async_copy(f.at[pl.ds(1, count)], front_out, store.at[0])
    write.start()
    wait_deep(LO_FB, HI_FB)
    for q, i in enumerate((b, inner)):
        lo[2, i] = lo_b[1, q]
        hi[2, i] = hi_b[1, q]
    for h in range(CHUNKS):
        wait_far(FAR_F + h)
    pair((pairs - 1) * core, 0)
    start_spread(1)
    comp[d] = part[d]

    def composite(p, carry):
        total = jnp.zeros((3, 128), jnp.float32)
        clear = jnp.ones((1, 128), jnp.float32)
        for s in range(depths):
            block = comp[s, p]
            total = total + clear * block[:3]
            clear = clear * block[3:]
        result[p] = jnp.concatenate([total, clear], axis=0)
        return carry

    end_spread(0)
    lax.fori_loop(1 - core, pairs - core, composite, 0)
    end_spread(1)
    composite((pairs - 1) * core, 0)
    for p in range(pairs):
        tile = result[p]
        other = pltpu.roll(tile, 64, 1)
        for v in range(4):
            picture[v, 2 * p : 2 * p + 1] = tile[v : v + 1, :64]
            picture[v, 2 * p + 1 : 2 * p + 2] = other[v : v + 1, :64]

    for copy, there in started.values():
        if there is None:
            copy.wait_send()
        else:
            pl.when(there)(copy.wait_send)

    def sent(k, carry):
        for stage in range(2):
            spread(stage, k).wait_send()
        return carry

    lax.fori_loop(1, depths, sent, 0)
    write.wait()


def shards(rows, depths, field, diffusivity, velocity):
    count, deep, width = field.shape
    row = (deep, width)
    f32 = jnp.float32
    pairs = count // 2
    any_space = pl.BlockSpec(memory_space=pl.ANY)
    vmem = pltpu.VMEM
    return pl.pallas_call(
        functools.partial(kernel, rows, depths, OPACITY_TOTAL / (deep * depths)),
        out_shape=(
            jax.ShapeDtypeStruct(field.shape, f32),
            jax.ShapeDtypeStruct((4, count, width // depths), f32),
        ),
        in_specs=[any_space] * 3,
        out_specs=(any_space, pl.BlockSpec(memory_space=pltpu.VMEM)),
        scratch_shapes=[
            vmem((count + 2,) + row, f32),
            vmem((count + 2,) + row, f32),
            vmem((count + 2,) + row, f32),
            vmem(diffusivity.shape, diffusivity.dtype),
            vmem(velocity.shape, velocity.dtype),
            vmem(row, f32), vmem(row, f32), vmem(row, f32), vmem(row, f32),
            vmem((3, count, 1, width), f32), vmem((3, count, 1, width), f32),
            vmem((3, count, 1, width), f32), vmem((3, count, 1, width), f32),
            vmem((2, 2, 1, width), f32), vmem((2, 2, 1, width), f32),
            vmem((2, 2, 1, width), f32), vmem((2, 2, 1, width), f32),
            vmem((depths, pairs, 4, 128), f32),
            vmem((depths, pairs, 4, 128), f32),
            vmem((pairs, 4, 128), f32),
            pltpu.SemaphoreType.DMA((3,)),
            pltpu.SemaphoreType.DMA((1,)),
            pltpu.SemaphoreType.DMA((COPIES,)),
            pltpu.SemaphoreType.DMA((COPIES,)),
            pltpu.SemaphoreType.DMA((2, depths)),
            pltpu.SemaphoreType.DMA((2, depths)),
            pltpu.SemaphoreType.REGULAR((2,)),
        ],
        compiler_params=pltpu.CompilerParams(collective_id=0, has_side_effects=True),
        name="front_and_rays",
    )(field, diffusivity, velocity)


def solution(mesh):
    return jax.shard_map(
        functools.partial(shards, mesh.shape["rows"], mesh.shape["depth"]),
        mesh=mesh,
        in_specs=(
            P("rows", "depth", None),
            P("rows", "depth", None),
            P(None, "rows", "depth", None),
        ),
        out_specs=(P("rows", "depth", None), P(None, "rows", "depth")),
        check_vma=False,
    )
```

time: 117 us -> 113 us (0.966)
  the two profiles are of different devices: /device:TPU:4 before, /device:TPU:24 now
where the time goes in v2:
time: 113 us
  Pallas kernels  109 us (96%)
  local copies, waits for them, and re-layouts  2.5 us (2%)
    pallas_call x1, Pallas kernels, shards(): pl.pallas_call(functools.partial(kernel, rows, depths, OPACITY_TOTAL / (d...  109 us
    unnamed x4, local copies, waits for them, and re-layouts  2.5 us

profile of v2, /device:TPU:24, one launch (start us, length us, event | category | flops | bytes accessed | tf_op | source)
XLA Modules:
  0.0 112.5 jit_solution(14007588234625744375)
XLA Ops:
  0.6 109.4 %front_and_rays.1 = (f32[8,16,1024]{2,1,0:T(8,128)}, f32[4,8,64]{2,1,0:T(8,128)}) custom-call(f32[8,16,1024]{2,1,0:T(8,128)} %field.1, bf16[8,16,1024]{2,1,0:T(8,128)(2,1)} %diffusivity.1, bf16[3,8,16,1024]{3,2,1,0:T(8,128)(2,1)} %velocity.1), custom_call_target="tpu_custom_call" | custom-call | tf_op jit(solution)/shard_map/front_and_rays/pallas_call | solution.py:399
  110.0 0.0 copy-start
  110.0 1.9 %copy.7 = f32[8,16,1024]{2,1,0:T(8,128)} copy(f32[8,16,1024]{2,1,0:T(8,128)} %get-tuple-element.4) | data formatting | bytes 1048576
  111.9 0.0 copy-done
  111.9 0.6 copy.8
Async XLA Ops:
  110.0 1.9 %copy-start = (f32[4,8,64]{2,1,0:T(8,128)S(1)}, f32[4,8,64]{2,1,0:T(8,128)}, u32[]{:S(2)}) copy-start(f32[4,8,64]{2,1,0:T(8,128)} %get-tuple-element.5) | copy-start | bytes 24580

commit v3 on v2

--- a/solution.py
+++ b/solution.py
@@ -13,11 +13,10 @@
 
 (NEAR_U, LO_U, HI_U, NEAR_M, LO_M, HI_M, NEAR_F, LO_F, HI_F,
  LO_MB, HI_MB, LO_FB, HI_FB, FAR_U) = range(14)
-SPLIT = 2
+SPLIT = 4
 CHUNKS = 2 * SPLIT
 FAR_M, FAR_F = FAR_U + CHUNKS, FAR_U + 2 * CHUNKS
 COPIES = FAR_U + 3 * CHUNKS
-
 
 def shifted(value, before, axis, low, high):
     size = value.shape[axis]
@@ -25,7 +24,6 @@
     if before:
         return jnp.where(index == 0, low, pltpu.roll(value, 1, axis))
     return jnp.where(index == size - 1, high, pltpu.roll(value, size - 1, axis))
-
 
 def section(ref, low, high, diff, vel, i):
     center, row_before, row_after = ref[i + 1], ref[i], ref[i + 2]
@@ -45,7 +43,6 @@
         flow = part if flow is None else flow + part
         total = total - (up - down)
     return center + TIME_STEP * (flow + center * (total - center))
-
 
 def ray_row(ref, low, high, i, opacity):
     center = ref[i + 1]
@@ -69,10 +66,9 @@
     blue = jnp.sum(weight - bright, axis=0, keepdims=True)
     return red, green, blue, jnp.exp(-through[size - 1 : size])
 
-
 def kernel(rows, depths, opacity, field, diffusivity, velocity, front_out, picture, u, m, f, diff,
            vel, coef, far_u, far_m, p_row, lo, hi, edge_lo, edge_hi, lo_b, hi_b,
-           edge_lo_b, edge_hi_b, part, comp, result, load, store, send, recv, send_a, recv_a, token):
+           edge_lo_b, edge_hi_b, part, comp, result, load, send, recv, send_a, recv_a, token):
     r, d = lax.axis_index("rows"), lax.axis_index("depth")
     core = r % 2
     count = field.shape[0]
@@ -236,35 +232,47 @@
         edges(i, 1, value)
         return carry
 
-    lax.fori_loop(0, count, first, 0)
-    start_deep(LO_M, HI_M)
-    start_near(NEAR_M)
+    first(b, 0)
+
+    def forward_middle():
+        for h, at in enumerate(chunk):
+            wait_far(FAR_U + h)
+            here = (b + 1,) + at
+            m[here] = m[here] + coef[at] * far_u[at]
+            if h == CHUNKS - 1:
+                edge_lo_b[0, 0] = m[b + 1, :1]
+                edge_hi_b[0, 0] = m[b + 1, u.shape[1] - 1 :]
+                start_deep(LO_MB, HI_MB)
+            start_far(FAR_M + h)
+
+    def other_rows():
+        lax.fori_loop(1 - core, count - core, first, 0)
+        start_deep(LO_M, HI_M)
+        start_near(NEAR_M)
+
+    pl.when(upper)(other_rows)
+    forward_middle()
+    pl.when(jnp.logical_not(upper))(other_rows)
     wait_near(NEAR_M)
     wait_deep(LO_M, HI_M)
 
+    def pass_token(way, there, on, onward):
+        @pl.when(there)
+        def _():
+            pl.semaphore_wait(token.at[way], 1)
+
+        @pl.when(on)
+        def _():
+            pl.semaphore_signal(token.at[way], inc=1, device_id=(r, onward), device_id_type=MESH)
+
     def line_entered():
-        for way, there, on, onward in ((0, has_lo, has_hi, d + 1), (1, has_hi, has_lo, d - 1)):
-            @pl.when(there)
+        ahead, back = (0, has_lo, has_hi, d + 1), (1, has_hi, has_lo, d - 1)
+        for half, order in ((d < depths // 2, (ahead, back)), (d >= depths // 2, (back, ahead))):
+            @pl.when(half)
             def _():
-                pl.semaphore_wait(token.at[way], 1)
-
-            @pl.when(on)
-            def _():
-                pl.semaphore_signal(
-                    token.at[way], inc=1, device_id=(r, onward), device_id_type=MESH
-                )
-
-    pl.when(upper)(line_entered)
-
-    for h, at in enumerate(chunk):
-        wait_far(FAR_U + h)
-        here = (b + 1,) + at
-        m[here] = m[here] + coef[at] * far_u[at]
-        if h == CHUNKS - 1:
-            edge_lo_b[0, 0] = m[b + 1, :1]
-            edge_hi_b[0, 0] = m[b + 1, u.shape[1] - 1 :]
-            start_deep(LO_MB, HI_MB)
-        start_far(FAR_M + h)
+                for way in order:
+                    pass_token(*way)
+
     wait_deep(LO_MB, HI_MB)
     lo[1, b] = lo_b[0, 0]
     hi[1, b] = hi_b[0, 0]
@@ -318,31 +326,27 @@
 
         lax.fori_loop(1, depths, body, 0)
 
-    def early_images():
-        lax.fori_loop(first_free, first_free + count - 2, second, 0)
-        start_deep(LO_F, HI_F)
-        start_near(NEAR_F)
-        value = section(m, lo.at[1], hi.at[1], diff, vel, inner)
-        f[inner + 1] = value
-        edge_lo_b[1, 1] = value[:1]
-        edge_hi_b[1, 1] = value[-1:]
-        pl.when(jnp.logical_not(upper))(line_entered)
-        wait_near(NEAR_F)
-        wait_deep(LO_F, HI_F)
-        lax.fori_loop(1 - core, pairs - core, pair, 0)
-        start_spread(0)
-
-    pl.when(jnp.logical_not(upper))(early_images)
+    lax.fori_loop(first_free, first_free + count - 2, second, 0)
+    start_deep(LO_F, HI_F)
+    start_near(NEAR_F)
+    value = section(m, lo.at[1], hi.at[1], diff, vel, inner)
+    f[inner + 1] = value
+    edge_lo_b[1, 1] = value[:1]
+    edge_hi_b[1, 1] = value[-1:]
+    pl.when(jnp.logical_not(upper))(line_entered)
     for h, at in enumerate(chunk):
         wait_far(FAR_M + h)
         f[(b + 1,) + at] = p_row[at] + coef[at] * far_m[at]
         start_far(FAR_F + h)
-    pl.when(upper)(early_images)
     edge_lo_b[1, 0] = f[b + 1, :1]
     edge_hi_b[1, 0] = f[b + 1, u.shape[1] - 1 :]
     start_deep(LO_FB, HI_FB)
-    write = pltpu.make_async_copy(f.at[pl.ds(1, count)], front_out, store.at[0])
-    write.start()
+    pl.when(upper)(line_entered)
+    wait_near(NEAR_F)
+    wait_deep(LO_F, HI_F)
+    lax.fori_loop(1 - core, pairs - core, pair, 0)
+    start_spread(0)
+    front_out[...] = f[1 : count + 1]
     wait_deep(LO_FB, HI_FB)
     for q, i in enumerate((b, inner)):
         lo[2, i] = lo_b[1, q]
@@ -386,8 +390,6 @@
         return carry
 
     lax.fori_loop(1, depths, sent, 0)
-    write.wait()
-
 
 def shards(rows, depths, field, diffusivity, velocity):
     count, deep, width = field.shape
@@ -399,11 +401,11 @@
     return pl.pallas_call(
         functools.partial(kernel, rows, depths, OPACITY_TOTAL / (deep * depths)),
         out_shape=(
-            jax.ShapeDtypeStruct(field.shape, f32),
-            jax.ShapeDtypeStruct((4, count, width // depths), f32),
+            pltpu.VMEM(field.shape, f32),
+            pltpu.VMEM((4, count, width // depths), f32),
         ),
         in_specs=[any_space] * 3,
-        out_specs=(any_space, pl.BlockSpec(memory_space=pltpu.VMEM)),
+        out_specs=(pl.BlockSpec(memory_space=pltpu.VMEM), pl.BlockSpec(memory_space=pltpu.VMEM)),
         scratch_shapes=[
             vmem((count + 2,) + row, f32),
             vmem((count + 2,) + row, f32),
@@ -419,7 +421,6 @@
             vmem((depths, pairs, 4, 128), f32),
             vmem((pairs, 4, 128), f32),
             pltpu.SemaphoreType.DMA((3,)),
-            pltpu.SemaphoreType.DMA((1,)),
             pltpu.SemaphoreType.DMA((COPIES,)),
             pltpu.SemaphoreType.DMA((COPIES,)),
             pltpu.SemaphoreType.DMA((2, depths)),
@@ -429,7 +430,6 @@
         compiler_params=pltpu.CompilerParams(collective_id=0, has_side_effects=True),
         name="front_and_rays",
     )(field, diffusivity, velocity)
-
 
 def solution(mesh):
     return jax.shard_map(

time: 113 us -> 100 us (0.88)
  Pallas kernels: 109 us -> 97 us
    pallas_call x1, Pallas kernels: 109 us -> 97 us  [shards(): pl.pallas_call(functools.partial(kernel, rows, depths, OPACITY_TOTAL / (d...]
    unnamed x4 -> x2, local copies, waits for them, and re-layouts: 2.5 us -> 1.4 us
where the time goes in v3:
time: 100 us; the launch traced here: 99.1 us
  Pallas kernels  97 us (97%)
  local copies, waits for them, and re-layouts  1.4 us (1%)
    pallas_call x1, Pallas kernels, shards(): pl.pallas_call(functools.partial(kernel, rows, depths, OPACITY_TOTAL / (d...  97 us

profile of v3, /device:TPU:24, one launch (start us, length us, event | category | flops | bytes accessed | tf_op | source)
XLA Modules:
  0.0 99.1 jit_solution(14758899750289657972)
XLA Ops:
  0.6 97.0 %front_and_rays.1 = (f32[8,16,1024]{2,1,0:T(8,128)S(1)}, f32[4,8,64]{2,1,0:T(8,128)S(1)}) custom-call(f32[8,16,1024]{2,1,0:T(8,128)} %field.1, bf16[8,16,1024]{2,1,0:T(8,128)(2,1)} %diffusivity.1, bf16[3,8,16,1024]{3,2,1,0:T(8,128)(2,1)} %velocity.1), custom_call_target="tpu_custom_call" | custom-call | tf_op jit(solution)/shard_map/front_and_rays/pallas_call | solution.py:401
  97.7 0.8 copy.7
  98.5 0.6 copy.8

commit v4 on v3

--- a/solution.py
+++ b/solution.py
@@ -16,7 +16,8 @@
 SPLIT = 4
 CHUNKS = 2 * SPLIT
 FAR_M, FAR_F = FAR_U + CHUNKS, FAR_U + 2 * CHUNKS
-COPIES = FAR_U + 3 * CHUNKS
+FAR_C = FAR_U + 3 * CHUNKS
+FAR_P, COPIES = FAR_C + 1, FAR_C + 2
 
 def shifted(value, before, axis, low, high):
     size = value.shape[axis]
@@ -67,7 +68,7 @@
     return red, green, blue, jnp.exp(-through[size - 1 : size])
 
 def kernel(rows, depths, opacity, field, diffusivity, velocity, front_out, picture, u, m, f, diff,
-           vel, coef, far_u, far_m, p_row, lo, hi, edge_lo, edge_hi, lo_b, hi_b,
+           vel, coef, far_u, far_c, far_m, far_p, p_row, lo, hi, edge_lo, edge_hi, lo_b, hi_b,
            edge_lo_b, edge_hi_b, part, comp, result, load, send, recv, send_a, recv_a, token):
     r, d = lax.axis_index("rows"), lax.axis_index("depth")
     core = r % 2
@@ -81,6 +82,8 @@
     near, far = r + 1 - 2 * core, r - 1 + 2 * core
     has_far = jnp.logical_and(far >= 0, far < rows)
     has_lo, has_hi = d > 0, d < depths - 1
+    whole = jnp.logical_and(has_far, d < 5 * depths // 8)
+    terms = jnp.logical_and(has_far, d >= 5 * depths // 8)
     upper = r // 2 % 2 == 1
     tiles = field.shape[2] // 128
 
@@ -156,7 +159,10 @@
     chunk = [
         (pl.ds(deep * p, deep), pl.ds(wide * q, wide)) for q in range(SPLIT) for p in range(2)
     ]
-    far_copies = {}
+    far_copies = {
+        FAR_C: remote(FAR_C, coef, far_c, (far, d)),
+        FAR_P: remote(FAR_P, p_row, far_p, (far, d)),
+    }
     for h, at in enumerate(chunk):
         for name, src, dst in (
             (FAR_U, u.at[(b + 1,) + at], far_u.at[at]),
@@ -188,17 +194,12 @@
 
     started = {}
 
-    def start_far(name):
-        started[name] = far_copies[name], has_far
-
-        @pl.when(has_far)
-        def _():
-            far_copies[name].start()
-
-    def wait_far(name):
-        @pl.when(has_far)
-        def _():
-            far_copies[name].wait_recv()
+    def start_far(name, there=has_far):
+        started[name] = far_copies[name], there
+        pl.when(there)(far_copies[name].start)
+
+    def wait_far(name, there=has_far):
+        pl.when(there)(far_copies[name].wait_recv)
 
     def start_near(name):
         started[name] = near_copies[name], None
@@ -225,6 +226,7 @@
         start_far(FAR_U + h)
     wait_near(NEAR_U)
     wait_deep(LO_U, HI_U)
+    start_far(FAR_C, terms)
 
     def first(i, carry):
         value = section(u, lo.at[0], hi.at[0], diff, vel, i)
@@ -277,6 +279,7 @@
     lo[1, b] = lo_b[0, 0]
     hi[1, b] = hi_b[0, 0]
     p_row[...] = section(m, lo.at[1], hi.at[1], diff, vel, b)
+    start_far(FAR_P, terms)
 
     def second(i, carry):
         value = section(m, lo.at[1], hi.at[1], diff, vel, i)
@@ -337,7 +340,7 @@
     for h, at in enumerate(chunk):
         wait_far(FAR_M + h)
         f[(b + 1,) + at] = p_row[at] + coef[at] * far_m[at]
-        start_far(FAR_F + h)
+        start_far(FAR_F + h, whole)
     edge_lo_b[1, 0] = f[b + 1, :1]
     edge_hi_b[1, 0] = f[b + 1, u.shape[1] - 1 :]
     start_deep(LO_FB, HI_FB)
@@ -352,7 +355,14 @@
         lo[2, i] = lo_b[1, q]
         hi[2, i] = hi_b[1, q]
     for h in range(CHUNKS):
-        wait_far(FAR_F + h)
+        wait_far(FAR_F + h, whole)
+    wait_far(FAR_C, terms)
+    wait_far(FAR_P, terms)
+
+    @pl.when(terms)
+    def _():
+        f[far_slot] = far_p[...] + far_c[...] * m[b + 1]
+
     pair((pairs - 1) * core, 0)
     start_spread(1)
     comp[d] = part[d]
@@ -412,7 +422,7 @@
             vmem((count + 2,) + row, f32),
             vmem(diffusivity.shape, diffusivity.dtype),
             vmem(velocity.shape, velocity.dtype),
-            vmem(row, f32), vmem(row, f32), vmem(row, f32), vmem(row, f32),
+            vmem(row, f32), vmem(row, f32), vmem(row, f32), vmem(row, f32), vmem(row, f32), vmem(row, f32),
             vmem((3, count, 1, width), f32), vmem((3, count, 1, width), f32),
             vmem((3, count, 1, width), f32), vmem((3, count, 1, width), f32),
             vmem((2, 2, 1, width), f32), vmem((2, 2, 1, width), f32),

time: 100 us -> 96 us (0.960)
  Pallas kernels: 97 us -> 93.3 us
    pallas_call x1, Pallas kernels: 97 us -> 93.3 us  [shards(): pl.pallas_call(functools.partial(kernel, rows, depths, OPACITY_TOTAL / (d...]
where the time goes in v4:
time: 96 us; the launch traced here: 95.4 us
  Pallas kernels  93.3 us (97%)
  local copies, waits for them, and re-layouts  1.4 us (1%)
    pallas_call x1, Pallas kernels, shards(): pl.pallas_call(functools.partial(kernel, rows, depths, OPACITY_TOTAL / (d...  93.3 us

profile of v4, /device:TPU:24, one launch (start us, length us, event | category | flops | bytes accessed | tf_op | source)
XLA Modules:
  0.0 95.4 jit_solution(12911409538914317731)
XLA Ops:
  0.6 93.3 %front_and_rays.1 = (f32[8,16,1024]{2,1,0:T(8,128)S(1)}, f32[4,8,64]{2,1,0:T(8,128)S(1)}) custom-call(f32[8,16,1024]{2,1,0:T(8,128)} %field.1, bf16[8,16,1024]{2,1,0:T(8,128)(2,1)} %diffusivity.1, bf16[3,8,16,1024]{3,2,1,0:T(8,128)(2,1)} %velocity.1), custom_call_target="tpu_custom_call" | custom-call | tf_op jit(solution)/shard_map/front_and_rays/pallas_call | solution.py:411
  94.0 0.8 copy.7
  94.8 0.6 copy.8
